TPU v7x, 512 devices: a whole 4x4x16 slice. The times are simulated.
512 devices in a mesh: space: 32 (over z, core), tm: 16 (over y, x).
Axes of the slice: x: 4, y: 4, z: 16, core: 2. Of those that a mesh axis runs over, the one named last changes fastest.
Arguments:
- snapshots: bfloat16 [65536, 16384], P('space', 'tm'), may hold values from -6 to 6
- basis: bfloat16 [65536, 256], P(('space', 'tm')), may hold values from -0.0234375 to 0.0234375
- lengths: int32 [16, 64], P('tm'), may hold values from 1 to 61, as said below
- owners: int32 [16, 64], P('tm'), may hold values from 0 to 31, as said below
Outputs:
- gram_out: bfloat16 [16, 32, 392, 392], P('tm', 'space')
- target_out: bfloat16 [16, 32, 392, 256], P('tm', 'space')
Inputs may be any that keep to these rules, and one draw needn't show every extreme that they name: Each row of lengths sums to 1024. The trajectories that one owner holds in one row have 62 snapshots together at most, and in every row some owner holds exactly 62. `owners`: in every row each space index owns exactly two trajectories.
All inputs are finite; a program needn't handle non-finite values.
Results may differ from a plain program's by a relative error of at most 0.0057.
Values may be sent and summed in bfloat16 or wider, within the bound.
No kernel may reach another device: no remote copies, remote signals or barrier semaphores. Data moves between devices by JAX's collectives and lax.ppermute only.
A program may use at most 64 MiB of HBM per device.

v0:
```python
import jax
import jax.numpy as jnp
import numpy as np
from jax import lax
from jax.sharding import PartitionSpec as P

QM = 16


def slot_plan(length_row, owner_row, owner_count, capacity, snap_count):
    traj_end = jnp.cumsum(length_row)
    starts = traj_end - length_row
    snap_index = jnp.arange(snap_count, dtype=jnp.int32)
    member = (
        (snap_index[:, None] >= starts[None, :]) & (snap_index[:, None] < traj_end[None, :])
    ).astype(jnp.int32)
    snap_start = jnp.sum(member * starts[None, :], axis=1)
    snap_end = jnp.sum(member * traj_end[None, :], axis=1)
    snap_owner = jnp.sum(member * owner_row[None, :], axis=1)
    traj_index = jnp.arange(length_row.shape[0], dtype=jnp.int32)
    same_owner = owner_row[:, None] == owner_row[None, :]
    earlier = traj_index[None, :] < traj_index[:, None]
    offset = jnp.sum(jnp.where(same_owner & earlier, length_row[None, :], 0), axis=1)
    slot_index = jnp.sum(member * offset[None, :], axis=1) + snap_index - snap_start
    has_next = (snap_index + 1 < snap_end).astype(jnp.int32)
    destination = snap_owner * capacity + slot_index
    source_rows = jnp.full((owner_count * capacity,), -1, jnp.int32).at[destination].set(snap_index)
    live_rows = jnp.zeros((owner_count * capacity,), jnp.int32).at[destination].set(has_next)
    return (source_rows, live_rows)


def library(coords, live_slots, weight_scale):
    first_mode, second_mode = np.triu_indices(QM)
    products = coords[:, first_mode] * coords[:, second_mode]
    library_rows = jnp.concatenate([coords, products], axis=1).astype(jnp.bfloat16)
    successor = jnp.concatenate(
        [coords[1:], jnp.zeros((1, coords.shape[1]), jnp.float32)], axis=0
    ).astype(jnp.bfloat16)
    weighted = library_rows * live_slots[:, None].astype(jnp.bfloat16)
    dims = (((0,), (0,)), ((), ()))
    gram_matrix = (
        lax.dot_general(weighted, library_rows, dims, preferred_element_type=jnp.float32)
        * weight_scale
    )
    targets = (
        lax.dot_general(weighted, successor, dims, preferred_element_type=jnp.float32)
        * weight_scale
    )
    return (gram_matrix.astype(jnp.bfloat16), targets.astype(jnp.bfloat16))


def on_device(snapshots, basis, lengths, owners):
    dims = (((0,), (0,)), ((), ()))
    snap_count = snapshots.shape[1]
    gathered = lax.all_gather(basis, "tm", axis=0, tiled=True)
    partial_value = lax.dot_general(snapshots, gathered, dims, preferred_element_type=jnp.float32)
    owner_count = lax.axis_size("space")
    capacity = 2 * snap_count // owner_count - 2
    source_rows, live_rows = slot_plan(lengths[0], owners[0], owner_count, capacity, snap_count)
    own_index = lax.axis_index("space")
    mine = lax.dynamic_slice_in_dim(source_rows, own_index * capacity, capacity)
    summed = lax.psum(partial_value, "space")
    packed = jnp.take(summed, jnp.maximum(mine, 0), axis=0) * (mine >= 0)[:, None].astype(
        jnp.float32
    )
    live_slots = lax.dynamic_slice_in_dim(live_rows, own_index * capacity, capacity)
    gram_matrix, targets = library(packed, live_slots, owner_count / snap_count)
    return (gram_matrix[None, None], targets[None, None])


def solution(mesh):
    placed = (P("space", "tm"), P(("space", "tm"), None), P("tm", None), P("tm", None))
    return jax.shard_map(
        on_device,
        mesh=mesh,
        in_specs=placed,
        out_specs=(P("tm", "space", None, None), P("tm", "space", None, None)),
        check_vma=False,
    )
```

profile of v0, /device:TPU:1, one launch (start us, length us, event | category | flops | bytes accessed | tf_op | source)
XLA Modules:
  0.0 301.7 jit_solution(7914927873324652971)
XLA Ops:
  7.2 0.7 all-gather.2.cloned.1.call-update
  7.9 0.0 all-reduce.3.cloned.1.call-start
  7.9 0.7 copy.20
  8.7 0.1 reduce-window.4
  8.8 0.1 reduce
  8.9 0.9 select_reduce_fusion.4
  9.8 0.7 fusion.17
  10.5 0.8 select_reduce_fusion
  11.4 4.3 %scatter_custom_fusion.1 = s32[1984]{0:T(1024)S(1)} fusion(s32[1024]{0:T(1024)S(1)} %bitcast.28, s32[1024]{0:T(1024)S(1)} %fusion.16, s32[]{:T(128)} %constant.22.clone.1), kind=kCustom, calls=%fused_computation.35 | custom fusion | bytes 7940 | tf_op jit(solution)/shard_map/scatter | solution.py:28
  15.7 4.3 %scatter_custom_fusion = s32[1984]{0:T(1024)S(1)} fusion(s32[1024]{0:T(1024)S(1)} %bitcast.29, s32[1024]{0:T(1024)S(1)} %iota.19, s32[]{:T(128)} %constant.21.clone.1), kind=kCustom, calls=%fused_computation.37 | custom fusion | bytes 7940 | tf_op jit(solution)/shard_map/scatter | solution.py:27
  20.1 52.9 %all-gather.2.cloned.1.call-done = bf16[2048,256]{1,0:T(8,128)(2,1)} async-done(((bf16[128,256]{1,0:T(8,128)(2,1)}), bf16[2048,256]{1,0:T(8,128)(2,1)}) %all-gather.2.cloned.1.call-update) | async-done | bytes 1048592 | tf_op jit(solution)/shard_map/all_gather | solution.py:55
  72.9 4.8 %fusion.22 = f32[1024,256]{1,0:T(8,128)} fusion(bf16[2048,1024]{1,0:T(8,128)(2,1)} %param.8, bf16[2048,256]{1,0:T(8,128)(2,1)} %all-gather.2.cloned.1.call-done), kind=kOutput, calls=%fused_computation.51 | convolution fusion | flops 1073741824 | bytes 6291456 | tf_op jit(solution)/shard_map/dot_general | solution.py:56
  77.7 0.1 dynamic-slice_convert_fusion
  77.8 0.1 broadcast_compare_fusion
  77.9 211.2 %all-reduce.3.cloned.1.call-done = f32[1024,256]{1,0:T(8,128)} async-done(((f32[1024,256]{1,0:T(8,128)}), f32[1024,256]{1,0:T(8,128)}) %all-reduce.3.cloned.1.call-update) | async-done | bytes 1048592 | tf_op jit(solution)/shard_map/psum | solution.py:62
  289.2 1.9 gather_fusion
  291.0 0.1 fusion.21
  291.1 0.1 copy.21
  291.2 0.7 gather_fusion.2
  291.9 0.7 gather_fusion.1
  292.6 0.1 copy.23
  292.7 0.1 copy.24
  292.8 1.1 fusion.1
  293.9 1.0 fusion.3
  (15 shorter events, 0.1 us)
Async XLA Ops:
  7.2 65.8 %all-gather.2.cloned.1.call-start = ((), (), s32[]{:S(2)}) async-start(), calls=%async_computation | async-start | bytes 1114112 | tf_op jit(solution)/shard_map/all_gather | solution.py:55
  7.9 281.3 %all-reduce.3.cloned.1.call-start = ((), (), s32[]{:S(2)}) async-start(), calls=%async_computation.1 | async-start | bytes 2097152 | tf_op jit(solution)/shard_map/psum | solution.py:62
  20.0 57.8 %copy-start.1 = (s32[136]{0:T(256)S(1)}, s32[136]{0:T(256)}, u32[]{:S(2)}) copy-start(s32[136]{0:T(256)} %constant.68) | copy-start | bytes 1636
  20.1 57.8 %copy-start = (s32[136]{0:T(256)S(1)}, s32[136]{0:T(256)}, u32[]{:S(2)}) copy-start(s32[136]{0:T(256)} %constant.69) | copy-start | bytes 1636
Sparse Core Ops, SparseCore 0:
  11.0 61.8 all-gather.1
  77.8 211.2 all-reduce.2
where the time goes:
time: 302 us
  waiting for transfers between devices  265 us (88%)
  between operations  14.2 us (5%)
  local copies, waits for them, and re-layouts  12.9 us (4%)
  matrix products  6.86 us (2%)
    psum x1, waiting for transfers between devices, on_device(): summed = lax.psum(partial_value, 'space')  211 us
    all_gather x1, waiting for transfers between devices, on_device(): gathered = lax.all_gather(basis, 'tm', axis=0, tiled=True)  52.9 us
  transfers between devices with their start and end apart: 2, of which 2 were waited for; matrix products, arithmetic and copies ran while one was open for 4% of the time, Pallas kernels for 0%

commit v1 on v0

--- a/solution.py
+++ b/solution.py
@@ -52,7 +52,9 @@
 def on_device(snapshots, basis, lengths, owners):
     dims = (((0,), (0,)), ((), ()))
     snap_count = snapshots.shape[1]
-    gathered = lax.all_gather(basis, "tm", axis=0, tiled=True)
+    gathered = jnp.concatenate(
+        lax.all_to_all(jnp.stack([basis] * lax.axis_size("tm")), "tm", 0, 0), axis=0
+    )
     partial_value = lax.dot_general(snapshots, gathered, dims, preferred_element_type=jnp.float32)
     owner_count = lax.axis_size("space")
     capacity = 2 * snap_count // owner_count - 2

time: 302 us -> 263 us (0.87)
  waiting for transfers between devices: 265 us -> 216 us
  starting transfers between devices: 0.08 us -> 7.63 us
    all_gather x1 -> x0, waiting for transfers between devices: 52.9 us -> none  [on_device(): gathered = lax.all_gather(basis, 'tm', axis=0, tiled=True)]
    all_to_all x0 -> x1, starting transfers between devices: none -> 7.58 us  [on_device(): lax.all_to_all(jnp.stack([basis] * lax.axis_size('tm')), 'tm', 0, 0)]
  transfers between devices with their start and end apart: 2 -> 2, of which waited for: 2 -> 2; matrix products, arithmetic and copies ran while one was open for 4% -> 5% of each run, Pallas kernels for 0% -> 0%
where the time goes in v1:
time: 263 us
  waiting for transfers between devices  216 us (82%)
  local copies, waits for them, and re-layouts  14.8 us (6%)
  between operations  14.2 us (5%)
  starting transfers between devices  7.63 us (3%)
  matrix products  6.63 us (3%)
  other arithmetic  2.93 us (1%)
    psum x1, waiting for transfers between devices, on_device(): summed = lax.psum(partial_value, 'space')  214 us
    all_to_all x1, starting transfers between devices, on_device(): lax.all_to_all(jnp.stack([basis] * lax.axis_size('tm')), 'tm', 0, 0)  7.58 us
  transfers between devices with their start and end apart: 2, of which 2 were waited for; matrix products, arithmetic and copies ran while one was open for 5% of the time, Pallas kernels for 0%

profile of v1, /device:TPU:1, one launch (start us, length us, event | category | flops | bytes accessed | tf_op | source)
XLA Modules:
  0.0 262.6 jit_solution(4654364162013349227)
XLA Ops:
  7.2 1.9 stack.2
  9.1 7.6 %all-to-all-start = ((bf16[16,128,256]{2,1,0:T(8,128)(2,1)}), bf16[16,128,256]{2,1,0:T(8,128)(2,1)S(1)}, u32[]{:S(2)}, u32[]{:S(2)}) async-start(bf16[16,128,256]{2,1,0:T(8,128)(2,1)} %stack.2), calls=%async_computation | async-start | bytes 2097152 | tf_op jit(solution)/shard_map/all_to_all | solution.py:56
  16.7 0.7 copy.20
  17.5 0.1 reduce-window.4
  17.6 0.1 reduce
  17.7 0.9 select_reduce_fusion.4
  18.6 0.7 fusion.17
  19.3 0.8 select_reduce_fusion
  20.2 4.3 %scatter_custom_fusion.1 = s32[1984]{0:T(1024)S(1)} fusion(s32[1024]{0:T(1024)S(1)} %bitcast.28, s32[1024]{0:T(1024)S(1)} %fusion.16, s32[]{:T(128)} %constant.22.clone.1), kind=kCustom, calls=%fused_computation.35 | custom fusion | bytes 7940 | tf_op jit(solution)/shard_map/scatter | solution.py:28
  24.5 4.3 %scatter_custom_fusion = s32[1984]{0:T(1024)S(1)} fusion(s32[1024]{0:T(1024)S(1)} %bitcast.29, s32[1024]{0:T(1024)S(1)} %iota.19, s32[]{:T(128)} %constant.21.clone.1), kind=kCustom, calls=%fused_computation.37 | custom fusion | bytes 7940 | tf_op jit(solution)/shard_map/scatter | solution.py:27
  28.8 2.3 all-to-all-done
  31.2 4.5 %fusion.22 = f32[1024,256]{1,0:T(8,128)} fusion(bf16[2048,1024]{1,0:T(8,128)(2,1)} %param.8, bf16[2048,256]{1,0:T(8,128)(2,1)S(1)} %bitcast.22), kind=kOutput, calls=%fused_computation.51 | convolution fusion | flops 1073741824 | bytes 6291456 | tf_op jit(solution)/shard_map/dot_general | solution.py:58
  35.7 0.1 dynamic-slice_convert_fusion
  35.8 0.1 broadcast_compare_fusion
  35.9 214.1 %all-reduce.3.cloned.1.call-done = f32[1024,256]{1,0:T(8,128)} async-done(((f32[1024,256]{1,0:T(8,128)}), f32[1024,256]{1,0:T(8,128)}) %all-reduce.3.cloned.1.call-update) | async-done | bytes 1048592 | tf_op jit(solution)/shard_map/psum | solution.py:64
  250.0 1.9 gather_fusion
  251.9 0.1 fusion.21
  252.0 0.1 copy.21
  252.1 0.7 gather_fusion.1
  252.8 0.1 copy.23
  252.9 0.7 gather_fusion.2
  253.5 0.1 copy.24
  253.7 1.1 fusion.1
  254.8 1.0 fusion.3
  (15 shorter events, 0.1 us)
Async XLA Ops:
  9.1 22.1 %all-to-all-start = ((bf16[16,128,256]{2,1,0:T(8,128)(2,1)}), bf16[16,128,256]{2,1,0:T(8,128)(2,1)S(1)}, u32[]{:S(2)}, u32[]{:S(2)}) async-start(bf16[16,128,256]{2,1,0:T(8,128)(2,1)} %stack.2), calls=%async_computation | async-start | bytes 2097152 | tf_op jit(solution)/shard_map/all_to_all | solution.py:56
  16.7 233.3 %all-reduce.3.cloned.1.call-start = ((), (), s32[]{:S(2)}) async-start(), calls=%async_computation.1 | async-start | bytes 2097152 | tf_op jit(solution)/shard_map/psum | solution.py:64
  31.2 4.7 %copy-start.1 = (s32[136]{0:T(256)S(1)}, s32[136]{0:T(256)}, u32[]{:S(2)}) copy-start(s32[136]{0:T(256)} %constant.68) | copy-start | bytes 1636
  31.2 4.8 %copy-start = (s32[136]{0:T(256)S(1)}, s32[136]{0:T(256)}, u32[]{:S(2)}) copy-start(s32[136]{0:T(256)} %constant.69) | copy-start | bytes 1636
Sparse Core Ops, SparseCore 0:
  35.8 214.1 all-reduce.2
